TPU v7x, 32 devices: a whole 2x2x4 slice. The times are simulated.
32 devices in a mesh: dp: 8 (over y, x, core), tensor: 4 (over z).
Axes of the slice: x: 2, y: 2, z: 4, core: 2. Of those that a mesh axis runs over, the one named last changes fastest.
Arguments:
- tokens: bfloat16 [6144, 2048], P(('dp', 'tensor')), may hold values from -6 to 6
- cotangent: bfloat16 [6144, 2048], P(('dp', 'tensor')), may hold values from -6 to 6
- deal: int32 [6144], P(('dp', 'tensor')), may hold values from 0 to 6143, as said below
- segment: int32 [6144], P('dp'), may hold values from 0 to 3, as said below
- norm1_gain: float32 [2, 2048], replicated, may hold values from 0.5 to 1.5
- norm1_shift: float32 [2, 2048], replicated, may hold values from -1.25 to 1.25
- query_weight: bfloat16 [2, 2048, 2048], P(None, 'dp', 'tensor'), may hold values from -0.125 to 0.125
- query_bias: float32 [2, 2048], P(None, 'tensor'), may hold values from -3 to 3
- kv_weight: bfloat16 [2, 2048, 256], P(None, 'dp', 'tensor'), may hold values from -0.125 to 0.125
- value_bias: float32 [2, 128], replicated, may hold values from -0.3125 to 0.3125
- out_weight: bfloat16 [2, 2048, 2048], P(None, 'tensor', 'dp'), may hold values from -1.5 to 1.5
- out_bias: float32 [2, 2048], replicated, may hold values from -1.75 to 1.75
- norm2_gain: float32 [2, 2048], replicated, may hold values from 0.5 to 1.5
- norm2_shift: float32 [2, 2048], replicated, may hold values from -1.25 to 1.25
- up_weight: bfloat16 [2, 2048, 8192], P(None, 'dp', 'tensor'), may hold values from -0.125 to 0.125
- up_bias: float32 [2, 8192], P(None, 'tensor'), may hold values from -3 to 3
- down_weight: bfloat16 [2, 8192, 2048], P(None, 'tensor', 'dp'), may hold values from -0.0625 to 0.0625
- down_bias: float32 [2, 2048], replicated, may hold values from -1.75 to 1.75
Outputs:
- layer_out: bfloat16 [6144, 2048], P(('dp', 'tensor'))
- tokens_grad: bfloat16 [6144, 2048], P(('dp', 'tensor'))
- norm1_gain_grad: float32 [2, 2048], replicated
- norm1_shift_grad: float32 [2, 2048], replicated
- query_weight_grad: float32 [2, 2048, 2048], P(None, 'dp', 'tensor')
- query_bias_grad: float32 [2, 2048], P(None, 'tensor')
- kv_weight_grad: float32 [2, 2048, 256], P(None, 'dp', 'tensor')
- value_bias_grad: float32 [2, 128], replicated
- out_weight_grad: float32 [2, 2048, 2048], P(None, 'tensor', 'dp')
- out_bias_grad: float32 [2, 2048], replicated
- norm2_gain_grad: float32 [2, 2048], replicated
- norm2_shift_grad: float32 [2, 2048], replicated
- up_weight_grad: float32 [2, 2048, 8192], P(None, 'dp', 'tensor')
- up_bias_grad: float32 [2, 8192], P(None, 'tensor')
- down_weight_grad: float32 [2, 8192, 2048], P(None, 'tensor', 'dp')
- down_bias_grad: float32 [2, 2048], replicated
Inputs may be any that keep to these rules, and one draw needn't show every extreme that they name: deal is a permutation: input row i becomes working row deal[i]; rows of both orders are laid out over the devices in order, 192 a device; a row stays on a device of the same tensor index, and every device deals exactly 24 rows to each dp index. `segment`: within each group of 768 working rows the labels never fall; each run of equal labels is one sequence of 96 to 768 rows; the first group is one sequence of all its rows.
All inputs are finite; a program needn't handle non-finite values.
Results may differ from a plain program's by a relative error of at most 0.025.
Values may be sent and summed in bfloat16 or wider, within the bound.
No kernel may reach another device: no remote copies, remote signals or barrier semaphores. Data moves between devices by JAX's collectives and lax.ppermute only.
A program may use at most 256 MiB of HBM per device.

v0:
```python
import jax
import jax.numpy as jnp
from jax import lax
from jax.sharding import PartitionSpec as P

HEAD = 128
EPSILON = 1e-05


def layer_norm(values, scales, offsets):
    row_mean = jnp.mean(values, axis=-1, keepdims=True)
    centred = values - row_mean
    row_var = jnp.mean(centred * centred, axis=-1, keepdims=True)
    return centred * lax.rsqrt(row_var + EPSILON) * scales + offsets


def gelu_tanh(values):
    return jax.nn.gelu(values, approximate=True)


def matmul(left, right):
    return jnp.dot(left, right, preferred_element_type=jnp.float32)


def contract_rows(left, right):
    return lax.dot_general(
        left, right, (((0,), (0,)), ((), ())), preferred_element_type=jnp.float32
    )


def contract_cols(left, right):
    return lax.dot_general(
        left, right, (((1,), (1,)), ((), ())), preferred_element_type=jnp.float32
    )


def rows_gather(values):
    return lax.all_gather(values, "tensor", axis=0, tiled=True)


def grad_gather(values):
    return lax.all_gather(values, "tensor", axis=0, tiled=True)


def rows_scatter(left, right):
    return lax.psum_scatter(
        matmul(left, right).astype(jnp.bfloat16), "tensor", scatter_dimension=0, tiled=True
    ).astype(jnp.float32)


def grad_scatter(factor_pairs):
    running = None
    for gradient, weight in factor_pairs:
        product_piece = contract_cols(gradient, weight)
        running = product_piece if running is None else running + product_piece
    return lax.psum_scatter(
        running.astype(jnp.bfloat16), "tensor", scatter_dimension=0, tiled=True
    ).astype(jnp.float32)


def place_slice(values, full_width, tensor_rank):
    start_col = tensor_rank * values.shape[0]
    return lax.dynamic_update_slice(jnp.zeros((full_width,), jnp.float32), values, (start_col,))


def local(
    tokens,
    cotangent,
    deal,
    segment,
    norm1_gain,
    norm1_shift,
    query_weight,
    query_bias,
    kv_weight,
    value_bias,
    out_weight,
    out_bias,
    norm2_gain,
    norm2_shift,
    up_weight,
    up_bias,
    down_weight,
    down_bias,
):
    local_rows = tokens.shape[0]
    dp_count = lax.axis_size("dp")
    tensor_count = lax.axis_size("tensor")
    tensor_rank = lax.axis_index("tensor")
    slot_rows = local_rows // dp_count
    layer_total = query_weight.shape[0]
    group_rows = local_rows * tensor_count
    query_cols = query_weight.shape[2]
    pair_width = kv_weight.shape[2]
    hidden_cols = up_weight.shape[2]
    head_count = query_cols // HEAD
    score_scale = HEAD ** (-0.5)
    target_dev = deal // local_rows // tensor_count
    target_row = deal % local_rows
    dev_ids = jnp.arange(dp_count, dtype=jnp.int32)
    dev_match = (target_dev[:, None] == dev_ids[None, :]).astype(jnp.int32)
    earlier = jnp.cumsum(dev_match, axis=0) - dev_match
    slot_of = target_dev * slot_rows + jnp.sum(earlier * dev_match, axis=1)
    row_ids = jnp.arange(local_rows, dtype=jnp.int32)
    send_mask = row_ids[:, None] == slot_of[None, :]
    send_table = send_mask.astype(jnp.bfloat16)
    sent_place = jnp.sum(jnp.where(send_mask, target_row[None, :], 0), axis=1)
    arrived_place = lax.all_to_all(sent_place, "dp", split_axis=0, concat_axis=0, tiled=True)
    tokens_sent = matmul(send_table, tokens).astype(jnp.bfloat16)
    tangent_sent = matmul(send_table, cotangent).astype(jnp.bfloat16)
    tokens_come, tangent_come = (
        lax.all_to_all(tokens_sent, "dp", split_axis=0, concat_axis=0, tiled=True),
        lax.all_to_all(tangent_sent, "dp", split_axis=0, concat_axis=0, tiled=True),
    )
    place_table = (row_ids[:, None] == arrived_place[None, :]).astype(jnp.bfloat16)
    stream = matmul(place_table, tokens_come)
    tangent = matmul(place_table, tangent_come)
    places = jnp.arange(group_rows, dtype=jnp.int32)
    allowed = (places[None, :] <= places[:, None]) & (segment[:, None] == segment[None, :])
    saved = []
    kept_weights = []
    for layer_index in range(layer_total):
        w_query, w_pair, w_out, w_up, w_down = (
            lax.all_gather(query_weight[layer_index], "dp", axis=0, tiled=True),
            lax.all_gather(kv_weight[layer_index], "dp", axis=0, tiled=True),
            lax.all_gather(out_weight[layer_index], "dp", axis=1, tiled=True),
            lax.all_gather(up_weight[layer_index], "dp", axis=0, tiled=True),
            lax.all_gather(down_weight[layer_index], "dp", axis=1, tiled=True),
        )
        kept_weights.append(None)
        normed_one = layer_norm(stream, norm1_gain[layer_index], norm1_shift[layer_index]).astype(
            jnp.bfloat16
        )
        normed_all = rows_gather(normed_one)
        queries = (matmul(normed_all, w_query) + query_bias[layer_index]).astype(jnp.bfloat16)
        full_bias = jnp.concatenate([jnp.zeros((HEAD,), jnp.float32), value_bias[layer_index]])
        pair_bias = lax.dynamic_slice_in_dim(full_bias, tensor_rank * pair_width, pair_width)
        pair_local = (matmul(normed_all, w_pair) + pair_bias).astype(jnp.bfloat16)
        pair_all = lax.all_gather(pair_local, "tensor", axis=1, tiled=True)
        key_rows = pair_all[:, :HEAD]
        value_rows = pair_all[:, HEAD:]
        query_heads = jnp.transpose(queries.reshape(group_rows, head_count, HEAD), (1, 0, 2))

        def attend(query_one):
            scores = jnp.where(allowed, contract_cols(query_one, key_rows) * score_scale, -1e30)
            row_top = jnp.max(scores, axis=-1, keepdims=True)
            exp_score = jnp.exp(scores - row_top)
            row_total = jnp.sum(exp_score, axis=-1, keepdims=True)
            weights = (exp_score / row_total).astype(jnp.bfloat16)
            return (matmul(weights, value_rows), (row_top + jnp.log(row_total))[:, 0])

        head_outs, log_totals = lax.map(attend, query_heads)
        mixed = (
            jnp.transpose(head_outs, (1, 0, 2)).reshape(group_rows, query_cols).astype(jnp.bfloat16)
        )
        hidden_state = stream + rows_scatter(mixed, w_out) + out_bias[layer_index]
        normed_two = layer_norm(
            hidden_state, norm2_gain[layer_index], norm2_shift[layer_index]
        ).astype(jnp.bfloat16)
        normed_two_all = rows_gather(normed_two)
        pre_gelu = matmul(normed_two_all, w_up) + up_bias[layer_index]
        activation = gelu_tanh(pre_gelu).astype(jnp.bfloat16)
        saved.append(
            (
                stream,
                normed_all,
                queries,
                pair_all,
                log_totals,
                mixed,
                hidden_state,
                normed_two_all,
                pre_gelu,
                activation,
            )
        )
        stream = hidden_state + rows_scatter(activation, w_down) + down_bias[layer_index]
    layer_out = stream.astype(jnp.bfloat16)
    reduced_by_layer = [None] * layer_total
    small_by_layer = [None] * layer_total
    for layer_index in reversed(range(layer_total)):
        (
            stream_in,
            normed_all,
            queries,
            pair_all,
            log_totals,
            mixed,
            hidden_state,
            normed_two_all,
            pre_gelu,
            activation,
        ) = saved[layer_index]
        w_query, w_pair, w_out, w_up, w_down = (
            lax.all_gather(query_weight[layer_index], "dp", axis=0, tiled=True),
            lax.all_gather(kv_weight[layer_index], "dp", axis=0, tiled=True),
            lax.all_gather(out_weight[layer_index], "dp", axis=1, tiled=True),
            lax.all_gather(up_weight[layer_index], "dp", axis=0, tiled=True),
            lax.all_gather(down_weight[layer_index], "dp", axis=1, tiled=True),
        )
        key_rows = pair_all[:, :HEAD]
        value_rows = pair_all[:, HEAD:]
        branch_grad = tangent.astype(jnp.bfloat16)
        down_bias_part = jnp.sum(branch_grad.astype(jnp.float32), axis=0)
        branch_all = grad_gather(branch_grad)
        down_grad = contract_rows(activation, branch_all)
        act_grad = contract_cols(branch_all, w_down)
        pre_grad = jax.vjp(gelu_tanh, pre_gelu)[1](act_grad)[0].astype(jnp.bfloat16)
        up_bias_part = jnp.sum(pre_grad.astype(jnp.float32), axis=0)
        up_grad = contract_rows(normed_two_all, pre_grad)
        normed_two_grad = grad_scatter(((pre_grad, w_up),))
        norm_pull_two = jax.vjp(
            layer_norm, hidden_state, norm2_gain[layer_index], norm2_shift[layer_index]
        )[1]
        hidden_part, gain_two_part, shift_two_part = norm_pull_two(normed_two_grad)
        hidden_grad = tangent + hidden_part
        attn_grad = hidden_grad.astype(jnp.bfloat16)
        out_bias_part = jnp.sum(attn_grad.astype(jnp.float32), axis=0)
        attn_all = grad_gather(attn_grad)
        out_grad = contract_rows(mixed, attn_all)
        mixed_grad = contract_cols(attn_all, w_out).astype(jnp.bfloat16)
        query_heads = jnp.transpose(queries.reshape(group_rows, head_count, HEAD), (1, 0, 2))
        dout_heads = jnp.transpose(mixed_grad.reshape(group_rows, head_count, HEAD), (1, 0, 2))

        def attend_back(carried, inputs):
            query_one, dout_one, log_one = inputs
            scores = jnp.where(allowed, contract_cols(query_one, key_rows) * score_scale, -1e30)
            probs = jnp.exp(scores - log_one[:, None])
            prob_grad = contract_cols(dout_one, value_rows)
            inner = jnp.sum(probs * prob_grad, axis=-1, keepdims=True)
            score_grad = (probs * (prob_grad - inner) * score_scale).astype(jnp.bfloat16)
            key_acc = carried[0] + contract_rows(score_grad, query_one)
            value_acc = carried[1] + contract_rows(probs.astype(jnp.bfloat16), dout_one)
            return ((key_acc, value_acc), matmul(score_grad, key_rows))

        start_acc = (
            jnp.zeros((group_rows, HEAD), jnp.float32),
            jnp.zeros((group_rows, HEAD), jnp.float32),
        )
        (key_grad, value_grad), query_grads = lax.scan(
            attend_back, start_acc, (query_heads, dout_heads, log_totals)
        )
        query_grad = (
            jnp.transpose(query_grads, (1, 0, 2))
            .reshape(group_rows, query_cols)
            .astype(jnp.bfloat16)
        )
        query_bias_part = jnp.sum(query_grad.astype(jnp.float32), axis=0)
        pair_part = jnp.concatenate([key_grad, value_grad], axis=1)
        pair_grad = lax.psum_scatter(
            pair_part.astype(jnp.bfloat16), "tensor", scatter_dimension=1, tiled=True
        )
        pair_bias_part = jnp.sum(pair_grad.astype(jnp.float32), axis=0)
        query_w_grad = contract_rows(normed_all, query_grad)
        pair_w_grad = contract_rows(normed_all, pair_grad)
        normed_grad = grad_scatter(((query_grad, w_query), (pair_grad, w_pair)))
        norm_pull_one = jax.vjp(
            layer_norm, stream_in, norm1_gain[layer_index], norm1_shift[layer_index]
        )[1]
        stream_part, gain_one_part, shift_one_part = norm_pull_one(normed_grad)
        tangent = hidden_grad + stream_part
        small_by_layer[layer_index] = (
            gain_one_part,
            shift_one_part,
            place_slice(query_bias_part, query_cols * tensor_count, tensor_rank),
            place_slice(pair_bias_part, pair_width * tensor_count, tensor_rank),
            out_bias_part,
            gain_two_part,
            shift_two_part,
            place_slice(up_bias_part, hidden_cols * tensor_count, tensor_rank),
            down_bias_part,
        )
        reduced_by_layer[layer_index] = (
            lax.psum_scatter(
                query_w_grad.astype(jnp.bfloat16), "dp", scatter_dimension=0, tiled=True
            ).astype(jnp.float32),
            lax.psum_scatter(
                pair_w_grad.astype(jnp.bfloat16), "dp", scatter_dimension=0, tiled=True
            ).astype(jnp.float32),
            lax.psum_scatter(
                out_grad.astype(jnp.bfloat16), "dp", scatter_dimension=1, tiled=True
            ).astype(jnp.float32),
            lax.psum_scatter(
                up_grad.astype(jnp.bfloat16), "dp", scatter_dimension=0, tiled=True
            ).astype(jnp.float32),
            lax.psum_scatter(
                down_grad.astype(jnp.bfloat16), "dp", scatter_dimension=1, tiled=True
            ).astype(jnp.float32),
        )
    summed = [
        jnp.stack([reduced_by_layer[layer_index][member] for layer_index in range(layer_total)])
        for member in range(5)
    ]
    smalls = [
        jnp.stack([small_by_layer[layer_index][member] for layer_index in range(layer_total)])
        for member in range(9)
    ]
    (
        gain_one_sum,
        shift_one_sum,
        query_bias_sum,
        pair_bias_sum,
        out_bias_sum,
        gain_two_sum,
        shift_two_sum,
        up_bias_sum,
        down_bias_sum,
    ) = lax.psum(
        (
            smalls[0],
            smalls[1],
            smalls[2],
            smalls[3],
            smalls[4],
            smalls[5],
            smalls[6],
            smalls[7],
            smalls[8],
        ),
        ("dp", "tensor"),
    )
    query_bias_grad = lax.dynamic_slice_in_dim(
        query_bias_sum, tensor_rank * query_cols, query_cols, 1
    )
    up_bias_grad = lax.dynamic_slice_in_dim(up_bias_sum, tensor_rank * hidden_cols, hidden_cols, 1)
    value_bias_grad = pair_bias_sum[:, HEAD:]
    out_slots = contract_rows(place_table, layer_out).astype(jnp.bfloat16)
    grad_slots = contract_rows(place_table, tangent.astype(jnp.bfloat16)).astype(jnp.bfloat16)
    out_back, grad_back = (
        lax.all_to_all(out_slots, "dp", split_axis=0, concat_axis=0, tiled=True),
        lax.all_to_all(grad_slots, "dp", split_axis=0, concat_axis=0, tiled=True),
    )
    layer_rows = contract_rows(send_table, out_back).astype(jnp.bfloat16)
    token_rows = contract_rows(send_table, grad_back).astype(jnp.bfloat16)
    return (
        layer_rows,
        token_rows,
        gain_one_sum,
        shift_one_sum,
        summed[0],
        query_bias_grad,
        summed[1],
        value_bias_grad,
        summed[2],
        out_bias_sum,
        gain_two_sum,
        shift_two_sum,
        summed[3],
        up_bias_grad,
        summed[4],
        down_bias_sum,
    )


def solution(mesh):
    in_specs = (
        P(("dp", "tensor"), None),
        P(("dp", "tensor"), None),
        P(("dp", "tensor")),
        P("dp"),
        P(),
        P(),
        P(None, "dp", "tensor"),
        P(None, "tensor"),
        P(None, "dp", "tensor"),
        P(),
        P(None, "tensor", "dp"),
        P(),
        P(),
        P(),
        P(None, "dp", "tensor"),
        P(None, "tensor"),
        P(None, "tensor", "dp"),
        P(),
    )
    out_specs = (
        P(("dp", "tensor"), None),
        P(("dp", "tensor"), None),
        P(),
        P(),
        P(None, "dp", "tensor"),
        P(None, "tensor"),
        P(None, "dp", "tensor"),
        P(),
        P(None, "tensor", "dp"),
        P(),
        P(),
        P(),
        P(None, "dp", "tensor"),
        P(None, "tensor"),
        P(None, "tensor", "dp"),
        P(),
    )
    return jax.shard_map(local, mesh=mesh, in_specs=in_specs, out_specs=out_specs, check_vma=False)
```

profile of v0, /device:TPU:0, one launch (start us, length us, event | category | flops | bytes accessed | tf_op | source)
XLA Modules:
  0.0 2494.6 jit_solution(4482688082752972419)
XLA Ops:
  50.9 50.5 %all-gather.27.cloned.1.call-done = bf16[768,2048]{1,0:T(8,128)(2,1)} async-done(((bf16[192,2048]{1,0:T(8,128)(2,1)}), bf16[768,2048]{1,0:T(8,128)(2,1)}) %all-gather.27.cloned.1.call-update) | async-done | bytes 3145744 | tf_op jit(solution)/shard_map/all_gather | solution.py:38
  104.3 15.1 all_gather.73
  135.8 34.1 %while.56 = (s32[]{:T(128)}, bf16[4,768,128]{1,2,0:T(8,128)(2,1)S(1)}, f32[4,768]{1,0:T(4,128)}, bf16[4,768,128]{2,1,0:T(8,128)(2,1)S(1)}, bf16[768,128]{1,0:T(8...) while((s32[]{:T(128)}, ...), condition=%wide.region_9.10_spmd.clone, body=%wide.region_6.9_spmd.clone.sunk | while | flops 308477184 | bytes 8108645 | solution.py:152
  179.2 56.9 %reduce-scatter.25.cloned.1.call-done = bf16[192,2048]{1,0:T(8,128)(2,1)} async-done(((bf16[768,2048]{1,0:T(8,128)(2,1)}), bf16[192,2048]{1,0:T(8,128)(2,1)}) %reduce-scatter.25.cloned.1.call-update) | async-done | bytes 786448 | tf_op jit(solution)/shard_map/reduce_scatter | solution.py:46
  242.8 50.0 %all-gather.47.cloned.1.call-done = bf16[1,2048,2048]{2,1,0:T(8,128)(2,1)} async-done(((bf16[1,256,2048]{2,1,0:T(8,128)(2,1)}), bf16[1,2048,2048]{2,1,0:T(8,128)(2,1)}) %all-gather.47.cloned.1.call-update) | async-done | bytes 8388624 | tf_op jit(solution)/shard_map/all_gather | solution.py:127
  292.9 65.5 %all-gather.29.cloned.1.call-done = bf16[768,2048]{1,0:T(8,128)(2,1)} async-done(((bf16[192,2048]{1,0:T(8,128)(2,1)}), bf16[768,2048]{1,0:T(8,128)(2,1)}) %all-gather.29.cloned.1.call-update) | async-done | bytes 3145744 | tf_op jit(solution)/shard_map/all_gather | solution.py:38
  370.1 45.4 %all-gather.49.cloned.1.call-done = bf16[1,2048,2048]{2,1,0:T(8,128)(2,1)} async-done(((bf16[1,2048,256]{2,1,0:T(8,128)(2,1)}), bf16[1,2048,2048]{2,1,0:T(8,128)(2,1)}) %all-gather.49.cloned.1.call-update) | async-done | bytes 8388624 | tf_op jit(solution)/shard_map/all_gather | solution.py:128
  415.5 13.1 fusion.85
  430.0 59.0 %reduce-scatter.27.cloned.1.call-done = bf16[192,2048]{1,0:T(8,128)(2,1)} async-done(((bf16[768,2048]{1,0:T(8,128)(2,1)}), bf16[192,2048]{1,0:T(8,128)(2,1)}) %reduce-scatter.27.cloned.1.call-update) | async-done | bytes 786448 | tf_op jit(solution)/shard_map/reduce_scatter | solution.py:46
  504.0 14.9 all-gather.51.cloned.1.call-done
  518.9 65.5 %all-gather.31.cloned.1.call-done = bf16[768,2048]{1,0:T(8,128)(2,1)} async-done(((bf16[192,2048]{1,0:T(8,128)(2,1)}), bf16[768,2048]{1,0:T(8,128)(2,1)}) %all-gather.31.cloned.1.call-update) | async-done | bytes 3145744 | tf_op jit(solution)/shard_map/all_gather | solution.py:38
  594.3 15.1 all_gather.81
  611.0 33.6 %while.57 = (s32[]{:T(128)}, bf16[4,768,128]{1,2,0:T(8,128)(2,1)S(1)}, f32[4,768]{1,0:T(4,128)}, bf16[4,768,128]{2,1,0:T(8,128)(2,1)S(1)}, bf16[768,128]{1,0:T(8...) while((s32[]{:T(128)}, ...), condition=%wide.region_19.20_spmd.clone, body=%wide.region_16.19_spmd.clone.sunk | while | flops 308477184 | bytes 8108645 | solution.py:152
  651.2 57.8 %reduce-scatter.29.cloned.1.call-done = bf16[192,2048]{1,0:T(8,128)(2,1)} async-done(((bf16[768,2048]{1,0:T(8,128)(2,1)}), bf16[192,2048]{1,0:T(8,128)(2,1)}) %reduce-scatter.29.cloned.1.call-update) | async-done | bytes 786448 | tf_op jit(solution)/shard_map/reduce_scatter | solution.py:46
  712.6 22.7 all_to_all.57
  738.0 32.3 %all-gather.55.cloned.1.call-done = bf16[1,2048,2048]{2,1,0:T(8,128)(2,1)} async-done(((bf16[1,256,2048]{2,1,0:T(8,128)(2,1)}), bf16[1,2048,2048]{2,1,0:T(8,128)(2,1)}) %all-gather.55.cloned.1.call-update) | async-done | bytes 8388624 | tf_op jit(solution)/shard_map/all_gather | solution.py:127
  770.2 65.5 %all-gather.33.cloned.1.call-done = bf16[768,2048]{1,0:T(8,128)(2,1)} async-done(((bf16[192,2048]{1,0:T(8,128)(2,1)}), bf16[768,2048]{1,0:T(8,128)(2,1)}) %all-gather.33.cloned.1.call-update) | async-done | bytes 3145744 | tf_op jit(solution)/shard_map/all_gather | solution.py:38
  835.7 11.8 fusion.58
  847.5 52.4 %all-gather.35.cloned.1.call-done = bf16[768,2048]{1,0:T(8,128)(2,1)} async-done(((bf16[192,2048]{1,0:T(8,128)(2,1)}), bf16[768,2048]{1,0:T(8,128)(2,1)}) %all-gather.35.cloned.1.call-update) | async-done | bytes 3145744 | tf_op jit(solution)/shard_map/all_gather | solution.py:42
  899.9 56.9 %all-gather.57.cloned.1.call-done = bf16[1,2048,2048]{2,1,0:T(8,128)(2,1)} async-done(((bf16[1,2048,256]{2,1,0:T(8,128)(2,1)}), bf16[1,2048,2048]{2,1,0:T(8,128)(2,1)}) %all-gather.57.cloned.1.call-update) | async-done | bytes 8388624 | tf_op jit(solution)/shard_map/all_gather | solution.py:128
  956.9 15.4 convert_reduce_fusion
  982.1 60.4 %reduce-scatter.33.cloned.1.call-done = bf16[192,2048]{1,0:T(8,128)(2,1)} async-done(((bf16[768,2048]{1,0:T(8,128)(2,1)}), bf16[192,2048]{1,0:T(8,128)(2,1)}) %reduce-scatter.33.cloned.1.call-update) | async-done | bytes 786448 | tf_op jit(solution)/shard_map/reduce_scatter | solution.py:56
  1047.8 63.4 %all-gather.37.cloned.1.call-done = bf16[768,2048]{1,0:T(8,128)(2,1)} async-done(((bf16[192,2048]{1,0:T(8,128)(2,1)}), bf16[768,2048]{1,0:T(8,128)(2,1)}) %all-gather.37.cloned.1.call-update) | async-done | bytes 3145744 | tf_op jit(solution)/shard_map/all_gather | solution.py:42
  1116.9 44.3 %while.58 = (s32[]{:T(128)}, f32[768,128]{1,0:T(8,128)}, f32[768,128]{1,0:T(8,128)}, bf16[4,768,128]{1,2,0:T(8,128)(2,1)}, bf16[4,768,128]{2,1,0:T(8,128)(2,1)},...) while((s32[]{:T(128)}, f32[768,128]{1,0:T(8,128)}, ...), condition=%wide.region_29.30_spmd.clone, body=%wide.region_27.29_spmd.clone.sunk | while | flops 763034880 | bytes 28140772 | solution.py:240
  1170.0 13.7 reduce-scatter.61.cloned.1.call-done
  1189.3 58.6 %reduce-scatter.35.cloned.1.call-done = bf16[192,2048]{1,0:T(8,128)(2,1)} async-done(((bf16[768,2048]{1,0:T(8,128)(2,1)}), bf16[192,2048]{1,0:T(8,128)(2,1)}) %reduce-scatter.35.cloned.1.call-update) | async-done | bytes 786448 | tf_op jit(solution)/shard_map/reduce_scatter | solution.py:56
  1256.2 63.2 %all-gather.39.cloned.1.call-done = bf16[768,2048]{1,0:T(8,128)(2,1)} async-done(((bf16[192,2048]{1,0:T(8,128)(2,1)}), bf16[768,2048]{1,0:T(8,128)(2,1)}) %all-gather.39.cloned.1.call-update) | async-done | bytes 3145744 | tf_op jit(solution)/shard_map/all_gather | solution.py:42
  1319.4 14.7 convert_reduce_fusion.1
  1346.1 59.0 %reduce-scatter.37.cloned.1.call-done = bf16[192,2048]{1,0:T(8,128)(2,1)} async-done(((bf16[768,2048]{1,0:T(8,128)(2,1)}), bf16[192,2048]{1,0:T(8,128)(2,1)}) %reduce-scatter.37.cloned.1.call-update) | async-done | bytes 786448 | tf_op jit(solution)/shard_map/reduce_scatter | solution.py:56
  1411.3 63.4 %all-gather.41.cloned.1.call-done = bf16[768,2048]{1,0:T(8,128)(2,1)} async-done(((bf16[192,2048]{1,0:T(8,128)(2,1)}), bf16[768,2048]{1,0:T(8,128)(2,1)}) %all-gather.41.cloned.1.call-update) | async-done | bytes 3145744 | tf_op jit(solution)/shard_map/all_gather | solution.py:42
  1480.6 39.8 %while.59 = (s32[]{:T(128)}, f32[768,128]{1,0:T(8,128)}, f32[768,128]{1,0:T(8,128)}, bf16[4,768,128]{1,2,0:T(8,128)(2,1)}, bf16[4,768,128]{2,1,0:T(8,128)(2,1)},...) while((s32[]{:T(128)}, f32[768,128]{1,0:T(8,128)}, ...), condition=%wide.region_39.40_spmd.clone, body=%wide.region_37.39_spmd.clone.sunk | while | flops 763034880 | bytes 28927240 | solution.py:240
  1523.5 13.1 fusion.91
  1545.4 12.6 convolution_convert_fusion
  1558.7 12.6 convolution_convert_fusion.1
  1629.0 12.4 all-to-all-done.2
  1647.6 80.4 %all-reduce.7.cloned.1.call-done = f32[2,8192]{1,0:T(2,128)} async-done(((f32[2,8192]{1,0:T(2,128)}), f32[2,8192]{1,0:T(2,128)}) %all-reduce.7.cloned.1.call-update) | async-done | bytes 65552 | tf_op jit(solution)/shard_map/psum | solution.py:308
  1738.0 27.2 %reduce-scatter.47.cloned.1.call-done = bf16[256,64]{0,1:T(8,128)(2,1)} async-done(((bf16[2048,64]{0,1:T(8,128)(2,1)}), bf16[256,64]{0,1:T(8,128)(2,1)}) %reduce-scatter.47.cloned.1.call-update) | async-done | bytes 32784 | tf_op jit(solution)/shard_map/reduce_scatter | solution.py:277
  1765.2 36.9 %reduce-scatter.45.cloned.1.call-done = bf16[256,64]{0,1:T(8,128)(2,1)} async-done(((bf16[2048,64]{0,1:T(8,128)(2,1)}), bf16[256,64]{0,1:T(8,128)(2,1)}) %reduce-scatter.45.cloned.1.call-update) | async-done | bytes 32784 | tf_op jit(solution)/shard_map/reduce_scatter | solution.py:277
  1803.6 73.3 %reduce-scatter.59.cloned.1.call-done = bf16[2048,256]{1,0:T(8,128)(2,1)} async-done(((bf16[2048,2048]{1,0:T(8,128)(2,1)}), bf16[2048,256]{1,0:T(8,128)(2,1)}) %reduce-scatter.59.cloned.1.call-update) | async-done | bytes 1048592 | tf_op jit(solution)/shard_map/reduce_scatter | solution.py:286
  1876.9 75.0 %reduce-scatter.57.cloned.1.call-done = bf16[2048,256]{1,0:T(8,128)(2,1)} async-done(((bf16[2048,2048]{1,0:T(8,128)(2,1)}), bf16[2048,256]{1,0:T(8,128)(2,1)}) %reduce-scatter.57.cloned.1.call-update) | async-done | bytes 1048592 | tf_op jit(solution)/shard_map/reduce_scatter | solution.py:286
  1955.9 59.2 %reduce-scatter.39.cloned.1.call-done = bf16[192,2048]{1,0:T(8,128)(2,1)} async-done(((bf16[768,2048]{1,0:T(8,128)(2,1)}), bf16[192,2048]{1,0:T(8,128)(2,1)}) %reduce-scatter.39.cloned.1.call-update) | async-done | bytes 786448 | tf_op jit(solution)/shard_map/reduce_scatter | solution.py:56
  2024.5 65.4 %reduce-scatter.55.cloned.1.call-done = bf16[256,2048]{1,0:T(8,128)(2,1)} async-done(((bf16[2048,2048]{1,0:T(8,128)(2,1)}), bf16[256,2048]{1,0:T(8,128)(2,1)}) %reduce-scatter.55.cloned.1.call-update) | async-done | bytes 1048592 | tf_op jit(solution)/shard_map/reduce_scatter | solution.py:283
  2089.9 75.0 %reduce-scatter.53.cloned.1.call-done = bf16[256,2048]{1,0:T(8,128)(2,1)} async-done(((bf16[2048,2048]{1,0:T(8,128)(2,1)}), bf16[256,2048]{1,0:T(8,128)(2,1)}) %reduce-scatter.53.cloned.1.call-update) | async-done | bytes 1048592 | tf_op jit(solution)/shard_map/reduce_scatter | solution.py:283
  2168.8 40.7 %reduce-scatter.51.cloned.1.call-done = bf16[512,256]{1,0:T(8,128)(2,1)} async-done(((bf16[512,2048]{1,0:T(8,128)(2,1)}), bf16[512,256]{1,0:T(8,128)(2,1)}) %reduce-scatter.51.cloned.1.call-update) | async-done | bytes 262160 | tf_op jit(solution)/shard_map/reduce_scatter | solution.py:280
  2209.5 44.9 %reduce-scatter.49.cloned.1.call-done = bf16[512,256]{1,0:T(8,128)(2,1)} async-done(((bf16[512,2048]{1,0:T(8,128)(2,1)}), bf16[512,256]{1,0:T(8,128)(2,1)}) %reduce-scatter.49.cloned.1.call-update) | async-done | bytes 262160 | tf_op jit(solution)/shard_map/reduce_scatter | solution.py:280
  2257.2 41.6 %reduce-scatter.43.cloned.1.call-done = bf16[256,512]{1,0:T(8,128)(2,1)} async-done(((bf16[2048,512]{1,0:T(8,128)(2,1)}), bf16[256,512]{1,0:T(8,128)(2,1)}) %reduce-scatter.43.cloned.1.call-update) | async-done | bytes 262160 | tf_op jit(solution)/shard_map/reduce_scatter | solution.py:274
  2298.8 44.8 %reduce-scatter.41.cloned.1.call-done = bf16[256,512]{1,0:T(8,128)(2,1)} async-done(((bf16[2048,512]{1,0:T(8,128)(2,1)}), bf16[256,512]{1,0:T(8,128)(2,1)}) %reduce-scatter.41.cloned.1.call-update) | async-done | bytes 262160 | tf_op jit(solution)/shard_map/reduce_scatter | solution.py:274
  2345.6 130.5 %all-reduce.9.cloned.1.call-done = (f32[2,2048]{1,0:T(2,128)}, f32[2,2048]{1,0:T(2,128)}, f32[2,2048]{1,0:T(2,128)}, f32[2,256]{1,0:T(2,128)}, f32[2,2048]{1,0:T...) async-done(((f32[2,2048]{1,0:T(2,128)}, f32[2,2048]{1,0:T(2,128)}, f32[2,2048]{1,0:T(2,128)}, f32[2,256]{1,0:T(2,128)}, f32[2,2048]{1,0:T(2,128)}, ...) | async-done | bytes 116752 | tf_op jit(solution)/shard_map/psum | solution.py:308
  (632 shorter events, 470.6 us)
Async XLA Ops:
  9.0 703.2 %copy-start.63 = (s32[192]{0:T(256)}, s32[192]{0:T(256)S(1)}, u32[]{:S(2)}) copy-start(s32[192]{0:T(256)S(1)} %multiply_add_fusion.4) | copy-start | bytes 2308
  9.8 9.8 all-to-all-start
  19.5 16.1 all-to-all-start.1
  23.1 78.2 %all-gather.27.cloned.1.call-start = ((), (), s32[]{:S(2)}) async-start(), calls=%async_computation.25 | async-start | bytes 3932160 | tf_op jit(solution)/shard_map/all_gather | solution.py:38
  38.3 92.1 %all-gather.43.cloned.1.call-start = ((), (), s32[]{:S(2)}) async-start(), calls=%async_computation.52 | async-start | bytes 2359296 | tf_op jit(solution)/shard_map/all_gather | solution.py:124
  39.2 130.8 %all-gather.45.cloned.1.call-start = ((), (), s32[]{:S(2)}) async-start(), calls=%async_computation.53 | async-start | bytes 2359296 | tf_op jit(solution)/shard_map/all_gather | solution.py:126
  40.1 196.0 %reduce-scatter.25.cloned.1.call-start = ((), (), s32[]{:S(2)}) async-start(), calls=%async_computation.26 | async-start | bytes 3932160 | tf_op jit(solution)/shard_map/reduce_scatter | solution.py:46
  175.8 117.1 %all-gather.47.cloned.1.call-start = ((), (), s32[]{:S(2)}) async-start(), calls=%async_computation.54 | async-start | bytes 9437184 | tf_op jit(solution)/shard_map/all_gather | solution.py:127
  179.0 179.4 %all-gather.29.cloned.1.call-start = ((), (), s32[]{:S(2)}) async-start(), calls=%async_computation.27 | async-start | bytes 3932160 | tf_op jit(solution)/shard_map/all_gather | solution.py:38
  237.5 251.5 %copy-start.8 = (f32[192,2048]{1,0:T(8,128)}, f32[192,2048]{1,0:T(8,128)S(1)}, u32[]{:S(2)}) copy-start(f32[192,2048]{1,0:T(8,128)S(1)} %get-tuple-element.560) | copy-start | bytes 4718596
  239.2 176.3 %all-gather.49.cloned.1.call-start = ((), (), s32[]{:S(2)}) async-start(), calls=%async_computation.55 | async-start | bytes 9437184 | tf_op jit(solution)/shard_map/all_gather | solution.py:128
  242.3 246.7 %reduce-scatter.27.cloned.1.call-start = ((), (), s32[]{:S(2)}) async-start(), calls=%async_computation.28 | async-start | bytes 3932160 | tf_op jit(solution)/shard_map/reduce_scatter | solution.py:46
  242.8 714.0 %copy-start.104 = (f32[1,2048]{1,0:T(1,128)}, f32[1,2048]{1,0:T(1,128)S(1)}, u32[]{:S(2)}) copy-start(f32[1,2048]{1,0:T(1,128)S(1)} %get-tuple-element.585) | copy-start | bytes 24580
  428.6 90.3 %all-gather.51.cloned.1.call-start = ((), (), s32[]{:S(2)}) async-start(), calls=%async_computation.56 | async-start | bytes 2359296 | tf_op jit(solution)/shard_map/all_gather | solution.py:124
  429.3 155.0 %all-gather.31.cloned.1.call-start = ((), (), s32[]{:S(2)}) async-start(), calls=%async_computation.29 | async-start | bytes 3932160 | tf_op jit(solution)/shard_map/all_gather | solution.py:38
  492.2 152.5 %all-gather.53.cloned.1.call-start = ((), (), s32[]{:S(2)}) async-start(), calls=%async_computation.57 | async-start | bytes 2359296 | tf_op jit(solution)/shard_map/all_gather | solution.py:126
  492.9 216.2 %reduce-scatter.29.cloned.1.call-start = ((), (), s32[]{:S(2)}) async-start(), calls=%async_computation.30 | async-start | bytes 3932160 | tf_op jit(solution)/shard_map/reduce_scatter | solution.py:46
  650.4 119.8 %all-gather.55.cloned.1.call-start = ((), (), s32[]{:S(2)}) async-start(), calls=%async_computation.58 | async-start | bytes 9437184 | tf_op jit(solution)/shard_map/all_gather | solution.py:127
  651.2 184.6 %all-gather.33.cloned.1.call-start = ((), (), s32[]{:S(2)}) async-start(), calls=%async_computation.31 | async-start | bytes 3932160 | tf_op jit(solution)/shard_map/all_gather | solution.py:38
  710.5 334.4 %copy-start.6 = (f32[192,2048]{1,0:T(8,128)}, f32[192,2048]{1,0:T(8,128)S(1)}, u32[]{:S(2)}) copy-start(f32[192,2048]{1,0:T(8,128)S(1)} %get-tuple-element.556) | copy-start | bytes 4718596
  712.1 187.8 %all-gather.35.cloned.1.call-start = ((), (), s32[]{:S(2)}) async-start(), calls=%async_computation.33 | async-start | bytes 3932160 | tf_op jit(solution)/shard_map/all_gather | solution.py:42
  737.1 308.3 %copy-start.15 = (f32[192,2048]{1,0:T(8,128)}, f32[192,2048]{1,0:T(8,128)S(1)}, u32[]{:S(2)}) copy-start(f32[192,2048]{1,0:T(8,128)S(1)} %get-tuple-element.605) | copy-start | bytes 4718596
  737.2 219.7 %all-gather.57.cloned.1.call-start = ((), (), s32[]{:S(2)}) async-start(), calls=%async_computation.59 | async-start | bytes 9437184 | tf_op jit(solution)/shard_map/all_gather | solution.py:128
  737.7 304.7 %reduce-scatter.33.cloned.1.call-start = ((), (), s32[]{:S(2)}) async-start(), calls=%async_computation.34 | async-start | bytes 3932160 | tf_op jit(solution)/shard_map/reduce_scatter | solution.py:56
  982.0 129.1 %all-gather.37.cloned.1.call-start = ((), (), s32[]{:S(2)}) async-start(), calls=%async_computation.35 | async-start | bytes 3932160 | tf_op jit(solution)/shard_map/all_gather | solution.py:42
  1047.5 136.2 %reduce-scatter.61.cloned.1.call-start = ((), (), s32[]{:S(2)}) async-start(), calls=%async_computation.60 | async-start | bytes 491520
  1164.3 83.6 %reduce-scatter.35.cloned.1.call-start = ((), (), s32[]{:S(2)}) async-start(), calls=%async_computation.36 | async-start | bytes 3932160 | tf_op jit(solution)/shard_map/reduce_scatter | solution.py:56
  1189.3 130.1 %all-gather.39.cloned.1.call-start = ((), (), s32[]{:S(2)}) async-start(), calls=%async_computation.37 | async-start | bytes 3932160 | tf_op jit(solution)/shard_map/all_gather | solution.py:42
  1255.7 149.4 %reduce-scatter.37.cloned.1.call-start = ((), (), s32[]{:S(2)}) async-start(), calls=%async_computation.38 | async-start | bytes 3932160 | tf_op jit(solution)/shard_map/reduce_scatter | solution.py:56
  1346.0 128.7 %all-gather.41.cloned.1.call-start = ((), (), s32[]{:S(2)}) async-start(), calls=%async_computation.39 | async-start | bytes 3932160 | tf_op jit(solution)/shard_map/all_gather | solution.py:42
  1411.1 131.8 %reduce-scatter.63.cloned.1.call-start = ((), (), s32[]{:S(2)}) async-start(), calls=%async_computation.61 | async-start | bytes 491520
  1523.5 97.0 %reduce-scatter.31.cloned.1.call-start = ((), (), s32[]{:S(2)}) async-start(), calls=%async_computation.32 | async-start | bytes 3932160 | tf_op jit(solution)/shard_map/reduce_scatter | solution.py:46
  1536.7 191.2 %all-reduce.7.cloned.1.call-start = ((), (), s32[]{:S(2)}) async-start(), calls=%async_computation.49 | async-start | bytes 131072 | tf_op jit(solution)/shard_map/psum | solution.py:308
  1538.1 227.1 %reduce-scatter.47.cloned.1.call-start = ((), (), s32[]{:S(2)}) async-start(), calls=%async_computation.44 | async-start | bytes 294912 | tf_op jit(solution)/shard_map/reduce_scatter | solution.py:277
  1541.4 260.8 %reduce-scatter.45.cloned.1.call-start = ((), (), s32[]{:S(2)}) async-start(), calls=%async_computation.43 | async-start | bytes 294912 | tf_op jit(solution)/shard_map/reduce_scatter | solution.py:277
  1545.2 331.8 %reduce-scatter.59.cloned.1.call-start = ((), (), s32[]{:S(2)}) async-start(), calls=%async_computation.51 | async-start | bytes 9437184 | tf_op jit(solution)/shard_map/reduce_scatter | solution.py:286
  1558.0 393.9 %reduce-scatter.57.cloned.1.call-start = ((), (), s32[]{:S(2)}) async-start(), calls=%async_computation.50 | async-start | bytes 9437184 | tf_op jit(solution)/shard_map/reduce_scatter | solution.py:286
  1571.3 443.8 %reduce-scatter.39.cloned.1.call-start = ((), (), s32[]{:S(2)}) async-start(), calls=%async_computation.40 | async-start | bytes 3932160 | tf_op jit(solution)/shard_map/reduce_scatter | solution.py:56
  1578.7 511.2 %reduce-scatter.55.cloned.1.call-start = ((), (), s32[]{:S(2)}) async-start(), calls=%async_computation.48 | async-start | bytes 9437184 | tf_op jit(solution)/shard_map/reduce_scatter | solution.py:283
  1591.5 573.4 %reduce-scatter.53.cloned.1.call-start = ((), (), s32[]{:S(2)}) async-start(), calls=%async_computation.47 | async-start | bytes 9437184 | tf_op jit(solution)/shard_map/reduce_scatter | solution.py:283
  1604.2 605.2 %reduce-scatter.51.cloned.1.call-start = ((), (), s32[]{:S(2)}) async-start(), calls=%async_computation.46 | async-start | bytes 2359296 | tf_op jit(solution)/shard_map/reduce_scatter | solution.py:280
  1610.4 643.9 %reduce-scatter.49.cloned.1.call-start = ((), (), s32[]{:S(2)}) async-start(), calls=%async_computation.45 | async-start | bytes 2359296 | tf_op jit(solution)/shard_map/reduce_scatter | solution.py:280
  1616.0 682.8 %reduce-scatter.43.cloned.1.call-start = ((), (), s32[]{:S(2)}) async-start(), calls=%async_computation.42 | async-start | bytes 2359296 | tf_op jit(solution)/shard_map/reduce_scatter | solution.py:274
  1624.3 17.1 all-to-all-start.2
  1628.8 714.8 %reduce-scatter.41.cloned.1.call-start = ((), (), s32[]{:S(2)}) async-start(), calls=%async_computation.41 | async-start | bytes 2359296 | tf_op jit(solution)/shard_map/reduce_scatter | solution.py:274
  2020.8 457.8 %all-to-all-start.4 = ((bf16[8,24,2048]{2,1,0:T(8,128)(2,1)}), bf16[8,24,2048]{2,1,0:T(8,128)(2,1)S(1)}, u32[]{:S(2)}, u32[]{:S(2)}) async-start(bf16[8,24,2048]{2,1,0:T(8,128)(2,1)} %bitcast.336), calls=%async_computation.12 | async-start | bytes 1572864 | tf_op jit(solution)/shard_map/all_to_all | solution.py:331
  2024.5 451.7 %all-reduce.9.cloned.1.call-start = ((), (), s32[]{:S(2)}) async-start(), calls=%async_computation.62 | async-start | bytes 233472 | tf_op jit(solution)/shard_map/psum | solution.py:308
  2254.4 233.5 %copy-start.1 = (bf16[192,2048]{1,0:T(8,128)(2,1)S(1)}, bf16[192,2048]{1,0:T(8,128)(2,1)}, u32[]{:S(2)}) copy-start(bf16[192,2048]{1,0:T(8,128)(2,1)} %param.26) | copy-start | bytes 2359300
  (130 other events, 2864.3 us)
Sparse Core Ops, SparseCore 0:
  38.4 62.8 all-gather.26
  103.8 26.5 all-gather.42
  132.8 28.1 all-gather.44
  175.9 60.1 reduce-scatter.24
  238.4 54.4 all-gather.46
  294.9 63.4 all-gather.28
  360.9 54.5 all-gather.48
  428.7 60.2 reduce-scatter.26
  490.9 27.9 all-gather.50
  520.9 63.4 all-gather.30
  586.3 26.8 all-gather.52
  650.5 58.4 reduce-scatter.28
  710.9 59.2 all-gather.54
  772.2 63.4 all-gather.32
  837.7 62.1 all-gather.34
  902.2 54.5 all-gather.56
  982.1 60.2 reduce-scatter.32
  1047.6 63.5 all-gather.36
  1164.4 19.2 reduce-scatter.60
  1189.4 58.5 reduce-scatter.34
  1255.8 63.5 all-gather.38
  1346.2 58.8 reduce-scatter.36
  1411.2 63.5 all-gather.40
  1523.6 19.2 reduce-scatter.62
  1545.7 58.5 reduce-scatter.30
  1610.3 117.5 all-reduce.6
  1730.8 34.3 reduce-scatter.46
  1768.5 33.5 reduce-scatter.44
  1805.6 71.2 reduce-scatter.58
  1880.6 71.2 reduce-scatter.56
  1954.8 60.2 reduce-scatter.38
  2018.6 71.2 reduce-scatter.54
  2093.6 71.2 reduce-scatter.52
  2168.2 41.2 reduce-scatter.50
  2213.1 41.2 reduce-scatter.48
  2257.5 41.2 reduce-scatter.42
  2302.2 41.2 reduce-scatter.40
  2351.1 124.9 all-reduce.8
where the time goes:
time: 2510 us; the launch traced here: 2490 us
  waiting for transfers between devices  1890 us (75%)
  matrix products  350 us (14%)
  other arithmetic  79.2 us (3%)
  blocking collectives  72.6 us (3%)
  local copies, waits for them, and re-layouts  65.7 us (3%)
    all_gather x4, waiting for transfers between devices, rows_gather(): return lax.all_gather(values, 'tensor', axis=0, tiled=True)  247 us
    all_gather x4, waiting for transfers between devices, grad_gather(): return lax.all_gather(values, 'tensor', axis=0, tiled=True)  242 us
    reduce_scatter x4, waiting for transfers between devices, grad_scatter(): lax.psum_scatter(running.astype(jnp.bfloat16), 'tensor', scatter_dimensio...  237 us
    psum x2, waiting for transfers between devices, local(): lax.psum((smalls[0], smalls[1], smalls[2], smalls[3], smalls[4], smalls[5...  211 us
    reduce_scatter x4, waiting for transfers between devices, rows_scatter(): lax.psum_scatter(matmul(left, right).astype(jnp.bfloat16), 'tensor', scat...  174 us
    reduce_scatter x2, waiting for transfers between devices, local(): lax.psum_scatter(down_grad.astype(jnp.bfloat16), 'dp', scatter_dimension=...  148 us
    reduce_scatter x2, waiting for transfers between devices, local(): lax.psum_scatter(up_grad.astype(jnp.bfloat16), 'dp', scatter_dimension=0,...  140 us
    dot_general x34, matrix products, contract_cols(): lax.dot_general(left, right, (((1,), (1,)), ((), ())), preferred_element_...  118 us
  transfers between devices with their start and end apart: 42, of which 38 were waited for; matrix products, arithmetic and copies ran while one was open for 11% of the time, Pallas kernels for 0%

commit v1 on v0

--- a/solution.py
+++ b/solution.py
@@ -124,7 +124,12 @@
             lax.all_gather(query_weight[layer_index], "dp", axis=0, tiled=True),
             lax.all_gather(kv_weight[layer_index], "dp", axis=0, tiled=True),
             lax.all_gather(out_weight[layer_index], "dp", axis=1, tiled=True),
-            lax.all_gather(up_weight[layer_index], "dp", axis=0, tiled=True),
+            jnp.concatenate(
+                lax.all_to_all(
+                    jnp.stack([up_weight[layer_index]] * lax.axis_size("dp")), "dp", 0, 0
+                ),
+                axis=0,
+            ),
             lax.all_gather(down_weight[layer_index], "dp", axis=1, tiled=True),
         )
         kept_weights.append(None)

time: 2510 us -> 2460 us (0.980)
  waiting for transfers between devices: 1890 us -> 1770 us
  blocking collectives: 72.6 us -> 164 us
    all_gather x4, waiting for transfers between devices: 247 us -> 123 us  [rows_gather(): return lax.all_gather(values, 'tensor', axis=0, tiled=True)]
    all_to_all x0 -> x1, waiting for transfers between devices: none -> 98.5 us  [local(): lax.all_to_all(jnp.stack([up_weight[layer_index]] * lax.axis_size('dp')),...]
    all_to_all x0 -> x1, blocking collectives: none -> 97.9 us  [local(): lax.all_to_all(jnp.stack([up_weight[layer_index]] * lax.axis_size('dp')),...]
    all_gather x4, waiting for transfers between devices: 242 us -> 189 us  [grad_gather(): return lax.all_gather(values, 'tensor', axis=0, tiled=True)]
    all_gather x2, waiting for transfers between devices: 102 us -> 63.3 us  [local(): lax.all_gather(down_weight[layer_index], 'dp', axis=1, tiled=True)]
  transfers between devices with their start and end apart: 42 -> 43, of which waited for: 38 -> 35; matrix products, arithmetic and copies ran while one was open for 11% -> 11% of each run, Pallas kernels for 0% -> 0%
where the time goes in v1:
time: 2460 us; the launch traced here: 2450 us
  waiting for transfers between devices  1770 us (72%)
  matrix products  331 us (13%)
  blocking collectives  164 us (7%)
  local copies, waits for them, and re-layouts  67.5 us (3%)
  other arithmetic  61.4 us (2%)
  starting transfers between devices  35.5 us (1%)
    reduce_scatter x4, waiting for transfers between devices, grad_scatter(): lax.psum_scatter(running.astype(jnp.bfloat16), 'tensor', scatter_dimensio...  238 us
    psum x2, waiting for transfers between devices, local(): lax.psum((smalls[0], smalls[1], smalls[2], smalls[3], smalls[4], smalls[5...  219 us
    all_gather x4, waiting for transfers between devices, grad_gather(): return lax.all_gather(values, 'tensor', axis=0, tiled=True)  189 us
    reduce_scatter x4, waiting for transfers between devices, rows_scatter(): lax.psum_scatter(matmul(left, right).astype(jnp.bfloat16), 'tensor', scat...  174 us
    reduce_scatter x2, waiting for transfers between devices, local(): lax.psum_scatter(up_grad.astype(jnp.bfloat16), 'dp', scatter_dimension=0,...  148 us
    reduce_scatter x2, waiting for transfers between devices, local(): lax.psum_scatter(down_grad.astype(jnp.bfloat16), 'dp', scatter_dimension=...  140 us
    all_gather x4, waiting for transfers between devices, rows_gather(): return lax.all_gather(values, 'tensor', axis=0, tiled=True)  123 us
    dot_general x34, matrix products, contract_cols(): lax.dot_general(left, right, (((1,), (1,)), ((), ())), preferred_element_...  117 us
  transfers between devices with their start and end apart: 43, of which 35 were waited for; matrix products, arithmetic and copies ran while one was open for 11% of the time, Pallas kernels for 0%

profile of v1, /device:TPU:0, one launch (start us, length us, event | category | flops | bytes accessed | tf_op | source)
XLA Modules:
  0.0 2449.9 jit_solution(12799499449724518346)
XLA Ops:
  26.4 14.2 all-to-all-done.1
  52.7 57.0 %all-gather.27.cloned.1.call-done = bf16[768,2048]{1,0:T(8,128)(2,1)} async-done(((bf16[192,2048]{1,0:T(8,128)(2,1)}), bf16[768,2048]{1,0:T(8,128)(2,1)}) %all-gather.27.cloned.1.call-update) | async-done | bytes 3145744 | tf_op jit(solution)/shard_map/all_gather | solution.py:38
  118.3 15.1 all_gather.71
  135.0 14.2 while.56
  155.5 57.9 %reduce-scatter.25.cloned.1.call-done = bf16[192,2048]{1,0:T(8,128)(2,1)} async-done(((bf16[768,2048]{1,0:T(8,128)(2,1)}), bf16[192,2048]{1,0:T(8,128)(2,1)}) %reduce-scatter.25.cloned.1.call-update) | async-done | bytes 786448 | tf_op jit(solution)/shard_map/reduce_scatter | solution.py:46
  243.9 98.5 %all-to-all-done.2 = bf16[8,256,2048]{2,1,0:T(8,128)(2,1)} async-done(((bf16[8,256,2048]{2,1,0:T(8,128)(2,1)}), bf16[8,256,2048]{2,1,0:T(8,128)(2,1)}, u32[]{:S(2)}, u32[]{:S(2)}) %all-to-all-start.2) | async-done | bytes 8388640 | tf_op jit(solution)/shard_map/all_to_all | solution.py:128
  363.9 13.1 fusion.78
  378.4 57.2 %reduce-scatter.27.cloned.1.call-done = bf16[192,2048]{1,0:T(8,128)(2,1)} async-done(((bf16[768,2048]{1,0:T(8,128)(2,1)}), bf16[192,2048]{1,0:T(8,128)(2,1)}) %reduce-scatter.27.cloned.1.call-update) | async-done | bytes 786448 | tf_op jit(solution)/shard_map/reduce_scatter | solution.py:46
  450.4 15.1 all-gather.49.cloned.1.call-done
  465.5 65.7 %all-gather.31.cloned.1.call-done = bf16[768,2048]{1,0:T(8,128)(2,1)} async-done(((bf16[192,2048]{1,0:T(8,128)(2,1)}), bf16[768,2048]{1,0:T(8,128)(2,1)}) %all-gather.31.cloned.1.call-update) | async-done | bytes 3145744 | tf_op jit(solution)/shard_map/all_gather | solution.py:38
  539.8 15.3 all_gather.78
  557.4 19.2 while.57
  582.1 58.4 %reduce-scatter.29.cloned.1.call-done = bf16[192,2048]{1,0:T(8,128)(2,1)} async-done(((bf16[768,2048]{1,0:T(8,128)(2,1)}), bf16[192,2048]{1,0:T(8,128)(2,1)}) %reduce-scatter.29.cloned.1.call-update) | async-done | bytes 786448 | tf_op jit(solution)/shard_map/reduce_scatter | solution.py:46
  644.1 16.0 all_to_all.67
  665.5 97.9 %all_to_all.68 = bf16[8,256,2048]{2,1,0:T(8,128)(2,1)} all-to-all(bf16[8,256,2048]{2,1,0:T(8,128)(2,1)S(1)} %stack.148), channel_id=1, replica_groups=mesh['dp'=8,'tensor'=4] {'dp'}, dimensions={0} | all-to-all | bytes 16777216 | tf_op jit(solution)/shard_map/all_to_all | solution.py:128
  763.4 11.7 fusion.192
  775.1 53.4 %all-gather.53.cloned.1.call-done = bf16[1,2048,2048]{2,1,0:T(8,128)(2,1)} async-done(((bf16[1,2048,256]{2,1,0:T(8,128)(2,1)}), bf16[1,2048,2048]{2,1,0:T(8,128)(2,1)}) %all-gather.53.cloned.1.call-update) | async-done | bytes 8388624 | tf_op jit(solution)/shard_map/all_gather | solution.py:133
  828.5 16.4 convert_reduce_fusion
  844.9 39.8 %all-gather.55.cloned.1.call-done = bf16[1,2048,2048]{2,1,0:T(8,128)(2,1)} async-done(((bf16[1,256,2048]{2,1,0:T(8,128)(2,1)}), bf16[1,2048,2048]{2,1,0:T(8,128)(2,1)}) %all-gather.55.cloned.1.call-update) | async-done | bytes 8388624 | tf_op jit(solution)/shard_map/all_gather | solution.py:203
  884.7 11.9 fusion.84
  896.7 60.4 %reduce-scatter.33.cloned.1.call-done = bf16[192,2048]{1,0:T(8,128)(2,1)} async-done(((bf16[768,2048]{1,0:T(8,128)(2,1)}), bf16[192,2048]{1,0:T(8,128)(2,1)}) %reduce-scatter.33.cloned.1.call-update) | async-done | bytes 786448 | tf_op jit(solution)/shard_map/reduce_scatter | solution.py:56
  962.3 63.4 %all-gather.37.cloned.1.call-done = bf16[768,2048]{1,0:T(8,128)(2,1)} async-done(((bf16[192,2048]{1,0:T(8,128)(2,1)}), bf16[768,2048]{1,0:T(8,128)(2,1)}) %all-gather.37.cloned.1.call-update) | async-done | bytes 3145744 | tf_op jit(solution)/shard_map/all_gather | solution.py:42
  1032.2 42.4 %while.58 = (s32[]{:T(128)}, f32[768,128]{1,0:T(8,128)}, f32[768,128]{1,0:T(8,128)}, bf16[4,768,128]{1,2,0:T(8,128)(2,1)}, bf16[4,768,128]{2,1,0:T(8,128)(2,1)},...) while((s32[]{:T(128)}, f32[768,128]{1,0:T(8,128)}, ...), condition=%wide.region_29.30_spmd.clone, body=%wide.region_27.29_spmd.clone.sunk | while | flops 763034880 | bytes 30498064 | solution.py:245
  1082.4 14.8 reduce-scatter.61.cloned.1.call-done
  1102.8 58.6 %reduce-scatter.35.cloned.1.call-done = bf16[192,2048]{1,0:T(8,128)(2,1)} async-done(((bf16[768,2048]{1,0:T(8,128)(2,1)}), bf16[192,2048]{1,0:T(8,128)(2,1)}) %reduce-scatter.35.cloned.1.call-update) | async-done | bytes 786448 | tf_op jit(solution)/shard_map/reduce_scatter | solution.py:56
  1170.2 62.7 %all-gather.39.cloned.1.call-done = bf16[768,2048]{1,0:T(8,128)(2,1)} async-done(((bf16[192,2048]{1,0:T(8,128)(2,1)}), bf16[768,2048]{1,0:T(8,128)(2,1)}) %all-gather.39.cloned.1.call-update) | async-done | bytes 3145744 | tf_op jit(solution)/shard_map/all_gather | solution.py:42
  1232.9 15.2 convert_reduce_fusion.1
  1248.1 39.9 %all-gather.57.cloned.1.call-done = bf16[1,2048,2048]{2,1,0:T(8,128)(2,1)} async-done(((bf16[1,256,2048]{2,1,0:T(8,128)(2,1)}), bf16[1,2048,2048]{2,1,0:T(8,128)(2,1)}) %all-gather.57.cloned.1.call-update) | async-done | bytes 8388624 | tf_op jit(solution)/shard_map/all_gather | solution.py:203
  1298.3 60.4 %reduce-scatter.37.cloned.1.call-done = bf16[192,2048]{1,0:T(8,128)(2,1)} async-done(((bf16[768,2048]{1,0:T(8,128)(2,1)}), bf16[192,2048]{1,0:T(8,128)(2,1)}) %reduce-scatter.37.cloned.1.call-update) | async-done | bytes 786448 | tf_op jit(solution)/shard_map/reduce_scatter | solution.py:56
  1364.5 63.2 %all-gather.41.cloned.1.call-done = bf16[768,2048]{1,0:T(8,128)(2,1)} async-done(((bf16[192,2048]{1,0:T(8,128)(2,1)}), bf16[768,2048]{1,0:T(8,128)(2,1)}) %all-gather.41.cloned.1.call-update) | async-done | bytes 3145744 | tf_op jit(solution)/shard_map/all_gather | solution.py:42
  1433.5 42.4 %while.59 = (s32[]{:T(128)}, f32[768,128]{1,0:T(8,128)}, f32[768,128]{1,0:T(8,128)}, bf16[4,768,128]{1,2,0:T(8,128)(2,1)}, bf16[4,768,128]{2,1,0:T(8,128)(2,1)},...) while((s32[]{:T(128)}, f32[768,128]{1,0:T(8,128)}, ...), condition=%wide.region_39.40_spmd.clone, body=%wide.region_37.39_spmd.clone.sunk | while | flops 763034880 | bytes 30498064 | solution.py:245
  1479.0 13.1 fusion.81
  1530.7 12.8 convolution_convert_fusion
  1544.2 12.6 convolution_convert_fusion.1
  1579.9 12.6 all-to-all-done.4
  1595.1 88.3 %all-reduce.7.cloned.1.call-done = f32[2,8192]{1,0:T(2,128)} async-done(((f32[2,8192]{1,0:T(2,128)}), f32[2,8192]{1,0:T(2,128)}) %all-reduce.7.cloned.1.call-update) | async-done | bytes 65552 | tf_op jit(solution)/shard_map/psum | solution.py:313
  1693.5 27.3 %reduce-scatter.47.cloned.1.call-done = bf16[256,64]{0,1:T(8,128)(2,1)} async-done(((bf16[2048,64]{0,1:T(8,128)(2,1)}), bf16[256,64]{0,1:T(8,128)(2,1)}) %reduce-scatter.47.cloned.1.call-update) | async-done | bytes 32784 | tf_op jit(solution)/shard_map/reduce_scatter | solution.py:282
  1720.8 36.9 %reduce-scatter.45.cloned.1.call-done = bf16[256,64]{0,1:T(8,128)(2,1)} async-done(((bf16[2048,64]{0,1:T(8,128)(2,1)}), bf16[256,64]{0,1:T(8,128)(2,1)}) %reduce-scatter.45.cloned.1.call-update) | async-done | bytes 32784 | tf_op jit(solution)/shard_map/reduce_scatter | solution.py:282
  1759.2 73.3 %reduce-scatter.55.cloned.1.call-done = bf16[256,2048]{1,0:T(8,128)(2,1)} async-done(((bf16[2048,2048]{1,0:T(8,128)(2,1)}), bf16[256,2048]{1,0:T(8,128)(2,1)}) %reduce-scatter.55.cloned.1.call-update) | async-done | bytes 1048592 | tf_op jit(solution)/shard_map/reduce_scatter | solution.py:288
  1832.5 75.0 %reduce-scatter.53.cloned.1.call-done = bf16[256,2048]{1,0:T(8,128)(2,1)} async-done(((bf16[2048,2048]{1,0:T(8,128)(2,1)}), bf16[256,2048]{1,0:T(8,128)(2,1)}) %reduce-scatter.53.cloned.1.call-update) | async-done | bytes 1048592 | tf_op jit(solution)/shard_map/reduce_scatter | solution.py:288
  1911.5 58.6 %reduce-scatter.39.cloned.1.call-done = bf16[192,2048]{1,0:T(8,128)(2,1)} async-done(((bf16[768,2048]{1,0:T(8,128)(2,1)}), bf16[192,2048]{1,0:T(8,128)(2,1)}) %reduce-scatter.39.cloned.1.call-update) | async-done | bytes 786448 | tf_op jit(solution)/shard_map/reduce_scatter | solution.py:56
  1979.5 65.4 %reduce-scatter.59.cloned.1.call-done = bf16[2048,256]{1,0:T(8,128)(2,1)} async-done(((bf16[2048,2048]{1,0:T(8,128)(2,1)}), bf16[2048,256]{1,0:T(8,128)(2,1)}) %reduce-scatter.59.cloned.1.call-update) | async-done | bytes 1048592 | tf_op jit(solution)/shard_map/reduce_scatter | solution.py:291
  2045.0 75.0 %reduce-scatter.57.cloned.1.call-done = bf16[2048,256]{1,0:T(8,128)(2,1)} async-done(((bf16[2048,2048]{1,0:T(8,128)(2,1)}), bf16[2048,256]{1,0:T(8,128)(2,1)}) %reduce-scatter.57.cloned.1.call-update) | async-done | bytes 1048592 | tf_op jit(solution)/shard_map/reduce_scatter | solution.py:291
  2123.8 40.7 %reduce-scatter.43.cloned.1.call-done = bf16[256,512]{1,0:T(8,128)(2,1)} async-done(((bf16[2048,512]{1,0:T(8,128)(2,1)}), bf16[256,512]{1,0:T(8,128)(2,1)}) %reduce-scatter.43.cloned.1.call-update) | async-done | bytes 262160 | tf_op jit(solution)/shard_map/reduce_scatter | solution.py:279
  2164.5 44.9 %reduce-scatter.41.cloned.1.call-done = bf16[256,512]{1,0:T(8,128)(2,1)} async-done(((bf16[2048,512]{1,0:T(8,128)(2,1)}), bf16[256,512]{1,0:T(8,128)(2,1)}) %reduce-scatter.41.cloned.1.call-update) | async-done | bytes 262160 | tf_op jit(solution)/shard_map/reduce_scatter | solution.py:279
  2212.2 41.6 %reduce-scatter.51.cloned.1.call-done = bf16[512,256]{1,0:T(8,128)(2,1)} async-done(((bf16[512,2048]{1,0:T(8,128)(2,1)}), bf16[512,256]{1,0:T(8,128)(2,1)}) %reduce-scatter.51.cloned.1.call-update) | async-done | bytes 262160 | tf_op jit(solution)/shard_map/reduce_scatter | solution.py:285
  2253.8 44.7 %reduce-scatter.49.cloned.1.call-done = bf16[512,256]{1,0:T(8,128)(2,1)} async-done(((bf16[512,2048]{1,0:T(8,128)(2,1)}), bf16[512,256]{1,0:T(8,128)(2,1)}) %reduce-scatter.49.cloned.1.call-update) | async-done | bytes 262160 | tf_op jit(solution)/shard_map/reduce_scatter | solution.py:285
  2300.6 130.6 %all-reduce.9.cloned.1.call-done = (f32[2,2048]{1,0:T(2,128)}, f32[2,2048]{1,0:T(2,128)}, f32[2,2048]{1,0:T(2,128)}, f32[2,256]{1,0:T(2,128)}, f32[2,2048]{1,0:T...) async-done(((f32[2,2048]{1,0:T(2,128)}, f32[2,2048]{1,0:T(2,128)}, f32[2,2048]{1,0:T(2,128)}, f32[2,256]{1,0:T(2,128)}, f32[2,2048]{1,0:T(2,128)}, ...) | async-done | bytes 116752 | tf_op jit(solution)/shard_map/psum | solution.py:313
  (615 shorter events, 426.3 us)
Async XLA Ops:
  7.2 45.5 %all-gather.43.cloned.1.call-start = ((), (), s32[]{:S(2)}) async-start(), calls=%async_computation.54 | async-start | bytes 2359296 | tf_op jit(solution)/shard_map/all_gather | solution.py:124
  10.9 632.7 %copy-start.54 = (s32[192]{0:T(256)}, s32[192]{0:T(256)S(1)}, u32[]{:S(2)}) copy-start(s32[192]{0:T(256)S(1)} %multiply_add_fusion.4) | copy-start | bytes 2308
  11.7 9.8 all-to-all-start
  21.5 19.1 all-to-all-start.1
  25.0 84.7 %all-gather.27.cloned.1.call-start = ((), (), s32[]{:S(2)}) async-start(), calls=%async_computation.27 | async-start | bytes 3932160 | tf_op jit(solution)/shard_map/all_gather | solution.py:38
  26.4 633.7 %copy-start.67 = (s32[192]{0:T(256)}, s32[192]{0:T(256)S(1)}, u32[]{:S(2)}) copy-start(s32[192]{0:T(256)S(1)} %eq.73) | copy-start | bytes 2308
  42.7 106.6 %all-gather.45.cloned.1.call-start = ((), (), s32[]{:S(2)}) async-start(), calls=%async_computation.55 | async-start | bytes 2359296 | tf_op jit(solution)/shard_map/all_gather | solution.py:126
  43.6 169.8 %reduce-scatter.25.cloned.1.call-start = ((), (), s32[]{:S(2)}) async-start(), calls=%async_computation.28 | async-start | bytes 3932160 | tf_op jit(solution)/shard_map/reduce_scatter | solution.py:46
  154.7 187.6 %all-gather.29.cloned.1.call-start = ((), (), s32[]{:S(2)}) async-start(), calls=%async_computation.29 | async-start | bytes 3932160 | tf_op jit(solution)/shard_map/all_gather | solution.py:38
  216.5 147.4 %all-gather.47.cloned.1.call-start = ((), (), s32[]{:S(2)}) async-start(), calls=%async_computation.56 | async-start | bytes 9437184 | tf_op jit(solution)/shard_map/all_gather | solution.py:133
  227.4 114.9 %all-to-all-start.2 = ((bf16[8,256,2048]{2,1,0:T(8,128)(2,1)}), bf16[8,256,2048]{2,1,0:T(8,128)(2,1)}, u32[]{:S(2)}, u32[]{:S(2)}) async-start(bf16[8,256,2048]{2,1,0:T(8,128)(2,1)} %stack.147), calls=%async_computation.3 | async-start | bytes 16777216 | tf_op jit(solution)/shard_map/all_to_all | solution.py:128
  232.6 203.1 %reduce-scatter.27.cloned.1.call-start = ((), (), s32[]{:S(2)}) async-start(), calls=%async_computation.30 | async-start | bytes 3932160 | tf_op jit(solution)/shard_map/reduce_scatter | solution.py:46
  243.9 584.6 %copy-start.95 = (f32[1,2048]{1,0:T(1,128)}, f32[1,2048]{1,0:T(1,128)S(1)}, u32[]{:S(2)}) copy-start(f32[1,2048]{1,0:T(1,128)S(1)} %get-tuple-element.587) | copy-start | bytes 24580
  377.0 88.5 %all-gather.49.cloned.1.call-start = ((), (), s32[]{:S(2)}) async-start(), calls=%async_computation.57 | async-start | bytes 2359296 | tf_op jit(solution)/shard_map/all_gather | solution.py:124
  377.8 153.4 %all-gather.31.cloned.1.call-start = ((), (), s32[]{:S(2)}) async-start(), calls=%async_computation.31 | async-start | bytes 3932160 | tf_op jit(solution)/shard_map/all_gather | solution.py:38
  438.7 138.0 %all-gather.51.cloned.1.call-start = ((), (), s32[]{:S(2)}) async-start(), calls=%async_computation.58 | async-start | bytes 2359296 | tf_op jit(solution)/shard_map/all_gather | solution.py:126
  439.3 201.2 %reduce-scatter.29.cloned.1.call-start = ((), (), s32[]{:S(2)}) async-start(), calls=%async_computation.32 | async-start | bytes 3932160 | tf_op jit(solution)/shard_map/reduce_scatter | solution.py:46
  582.0 181.4 %all-gather.33.cloned.1.call-start = ((), (), s32[]{:S(2)}) async-start(), calls=%async_computation.33 | async-start | bytes 3932160 | tf_op jit(solution)/shard_map/all_gather | solution.py:38
  641.9 317.5 %copy-start.6 = (f32[192,2048]{1,0:T(8,128)}, f32[192,2048]{1,0:T(8,128)S(1)}, u32[]{:S(2)}) copy-start(f32[192,2048]{1,0:T(8,128)S(1)} %get-tuple-element.556) | copy-start | bytes 4718596
  643.6 131.5 %all-gather.35.cloned.1.call-start = ((), (), s32[]{:S(2)}) async-start(), calls=%async_computation.35 | async-start | bytes 3932160 | tf_op jit(solution)/shard_map/all_gather | solution.py:42
  661.9 298.2 %copy-start.17 = (f32[192,2048]{1,0:T(8,128)}, f32[192,2048]{1,0:T(8,128)S(1)}, u32[]{:S(2)}) copy-start(f32[192,2048]{1,0:T(8,128)S(1)} %get-tuple-element.607) | copy-start | bytes 4718596
  661.9 166.6 %all-gather.53.cloned.1.call-start = ((), (), s32[]{:S(2)}) async-start(), calls=%async_computation.59 | async-start | bytes 9437184 | tf_op jit(solution)/shard_map/all_gather | solution.py:133
  662.5 222.2 %all-gather.55.cloned.1.call-start = ((), (), s32[]{:S(2)}) async-start(), calls=%async_computation.60 | async-start | bytes 9437184 | tf_op jit(solution)/shard_map/all_gather | solution.py:203
  663.1 293.9 %reduce-scatter.33.cloned.1.call-start = ((), (), s32[]{:S(2)}) async-start(), calls=%async_computation.36 | async-start | bytes 3932160 | tf_op jit(solution)/shard_map/reduce_scatter | solution.py:56
  896.6 129.1 %all-gather.37.cloned.1.call-start = ((), (), s32[]{:S(2)}) async-start(), calls=%async_computation.37 | async-start | bytes 3932160 | tf_op jit(solution)/shard_map/all_gather | solution.py:42
  962.1 135.1 %reduce-scatter.61.cloned.1.call-start = ((), (), s32[]{:S(2)}) async-start(), calls=%async_computation.62 | async-start | bytes 491520
  1077.8 83.6 %reduce-scatter.35.cloned.1.call-start = ((), (), s32[]{:S(2)}) async-start(), calls=%async_computation.38 | async-start | bytes 3932160 | tf_op jit(solution)/shard_map/reduce_scatter | solution.py:56
  1102.8 130.1 %all-gather.39.cloned.1.call-start = ((), (), s32[]{:S(2)}) async-start(), calls=%async_computation.39 | async-start | bytes 3932160 | tf_op jit(solution)/shard_map/all_gather | solution.py:42
  1169.2 118.8 %all-gather.57.cloned.1.call-start = ((), (), s32[]{:S(2)}) async-start(), calls=%async_computation.61 | async-start | bytes 9437184 | tf_op jit(solution)/shard_map/all_gather | solution.py:203
  1169.9 188.7 %reduce-scatter.37.cloned.1.call-start = ((), (), s32[]{:S(2)}) async-start(), calls=%async_computation.40 | async-start | bytes 3932160 | tf_op jit(solution)/shard_map/reduce_scatter | solution.py:56
  1298.3 129.5 %all-gather.41.cloned.1.call-start = ((), (), s32[]{:S(2)}) async-start(), calls=%async_computation.41 | async-start | bytes 3932160 | tf_op jit(solution)/shard_map/all_gather | solution.py:42
  1364.0 134.4 %reduce-scatter.63.cloned.1.call-start = ((), (), s32[]{:S(2)}) async-start(), calls=%async_computation.63 | async-start | bytes 491520
  1479.0 93.3 %reduce-scatter.31.cloned.1.call-start = ((), (), s32[]{:S(2)}) async-start(), calls=%async_computation.34 | async-start | bytes 3932160 | tf_op jit(solution)/shard_map/reduce_scatter | solution.py:46
  1492.2 191.3 %all-reduce.7.cloned.1.call-start = ((), (), s32[]{:S(2)}) async-start(), calls=%async_computation.51 | async-start | bytes 131072 | tf_op jit(solution)/shard_map/psum | solution.py:313
  1493.6 227.2 %reduce-scatter.47.cloned.1.call-start = ((), (), s32[]{:S(2)}) async-start(), calls=%async_computation.46 | async-start | bytes 294912 | tf_op jit(solution)/shard_map/reduce_scatter | solution.py:282
  1497.0 260.8 %reduce-scatter.45.cloned.1.call-start = ((), (), s32[]{:S(2)}) async-start(), calls=%async_computation.45 | async-start | bytes 294912 | tf_op jit(solution)/shard_map/reduce_scatter | solution.py:282
  1500.7 331.8 %reduce-scatter.55.cloned.1.call-start = ((), (), s32[]{:S(2)}) async-start(), calls=%async_computation.50 | async-start | bytes 9437184 | tf_op jit(solution)/shard_map/reduce_scatter | solution.py:288
  1512.3 395.2 %reduce-scatter.53.cloned.1.call-start = ((), (), s32[]{:S(2)}) async-start(), calls=%async_computation.49 | async-start | bytes 9437184 | tf_op jit(solution)/shard_map/reduce_scatter | solution.py:288
  1524.0 446.1 %reduce-scatter.39.cloned.1.call-start = ((), (), s32[]{:S(2)}) async-start(), calls=%async_computation.42 | async-start | bytes 3932160 | tf_op jit(solution)/shard_map/reduce_scatter | solution.py:56
  1530.5 514.5 %reduce-scatter.59.cloned.1.call-start = ((), (), s32[]{:S(2)}) async-start(), calls=%async_computation.53 | async-start | bytes 9437184 | tf_op jit(solution)/shard_map/reduce_scatter | solution.py:291
  1543.5 576.5 %reduce-scatter.57.cloned.1.call-start = ((), (), s32[]{:S(2)}) async-start(), calls=%async_computation.52 | async-start | bytes 9437184 | tf_op jit(solution)/shard_map/reduce_scatter | solution.py:291
  1556.8 607.7 %reduce-scatter.43.cloned.1.call-start = ((), (), s32[]{:S(2)}) async-start(), calls=%async_computation.44 | async-start | bytes 2359296 | tf_op jit(solution)/shard_map/reduce_scatter | solution.py:279
  1562.2 647.2 %reduce-scatter.41.cloned.1.call-start = ((), (), s32[]{:S(2)}) async-start(), calls=%async_computation.43 | async-start | bytes 2359296 | tf_op jit(solution)/shard_map/reduce_scatter | solution.py:279
  1566.6 687.2 %reduce-scatter.51.cloned.1.call-start = ((), (), s32[]{:S(2)}) async-start(), calls=%async_computation.48 | async-start | bytes 2359296 | tf_op jit(solution)/shard_map/reduce_scatter | solution.py:285
  1576.1 16.4 all-to-all-start.4
  1579.9 718.7 %reduce-scatter.49.cloned.1.call-start = ((), (), s32[]{:S(2)}) async-start(), calls=%async_computation.47 | async-start | bytes 2359296 | tf_op jit(solution)/shard_map/reduce_scatter | solution.py:285
  1975.8 457.9 %all-to-all-start.6 = ((bf16[8,24,2048]{2,1,0:T(8,128)(2,1)}), bf16[8,24,2048]{2,1,0:T(8,128)(2,1)S(1)}, u32[]{:S(2)}, u32[]{:S(2)}) async-start(bf16[8,24,2048]{2,1,0:T(8,128)(2,1)} %bitcast.341), calls=%async_computation.14 | async-start | bytes 1572864 | tf_op jit(solution)/shard_map/all_to_all | solution.py:336
  1979.5 451.7 %all-reduce.9.cloned.1.call-start = ((), (), s32[]{:S(2)}) async-start(), calls=%async_computation.64 | async-start | bytes 233472 | tf_op jit(solution)/shard_map/psum | solution.py:313
  (120 other events, 3420.4 us)
Sparse Core Ops, SparseCore 0:
  10.5 33.2 all-gather.42
  46.0 63.7 all-gather.26
  112.2 26.8 all-gather.44
  154.8 58.5 reduce-scatter.24
  216.6 63.5 all-gather.28
  282.5 81.3 all-gather.46
  377.1 58.4 reduce-scatter.26
  437.5 27.9 all-gather.48
  467.6 63.4 all-gather.30
  532.9 26.8 all-gather.50
  582.2 58.3 reduce-scatter.28
  643.7 63.5 all-gather.32
  709.4 62.1 all-gather.34
  773.9 54.5 all-gather.52
  830.2 54.3 all-gather.54
  896.7 60.2 reduce-scatter.32
  962.2 63.5 all-gather.36
  1077.9 19.2 reduce-scatter.60
  1102.9 58.5 reduce-scatter.34
  1169.3 63.4 all-gather.38
  1234.9 53.0 all-gather.56
  1298.4 60.2 reduce-scatter.36
  1364.2 63.5 all-gather.40
  1479.1 19.2 reduce-scatter.62
  1501.3 58.5 reduce-scatter.30
  1565.9 117.5 all-reduce.6
  1686.3 34.4 reduce-scatter.46
  1724.1 33.5 reduce-scatter.44
  1761.2 71.2 reduce-scatter.54
  1836.2 71.2 reduce-scatter.52
  1909.9 60.2 reduce-scatter.38
  1973.6 71.3 reduce-scatter.58
  2048.7 71.2 reduce-scatter.56
  2123.3 41.2 reduce-scatter.42
  2168.2 41.2 reduce-scatter.40
  2212.6 41.2 reduce-scatter.50
  2257.3 41.2 reduce-scatter.48
  2306.1 125.0 all-reduce.8
